TPU v7x, 32 devices: a whole 2x2x4 slice. The times are simulated.
32 devices in a mesh: tmpl: 2 (over core), row: 16 (over z, y, x).
Axes of the slice: x: 2, y: 2, z: 4, core: 2. Of those that a mesh axis runs over, the one named last changes fastest.
Arguments:
- pair_maps: bfloat16 [2, 2048, 2048, 64], P('tmpl', 'row'), may hold values from -6 to 6
- crop_tiles: int32 [2, 8], P('tmpl'), may hold values from 0 to 15, as said below
- full_length: int32 [1], replicated, may hold values from 1536 to 2048
- proj_weight: bfloat16 [2, 64, 320], replicated, may hold values from -0.75 to 0.75
- out_weight: bfloat16 [2, 64, 64], replicated, may hold values from -0.75 to 0.75
- final_weight: bfloat16 [64, 128], replicated, may hold values from -0.75 to 0.75
Outputs:
- embedding: bfloat16 [128, 1024, 1024], P(None, 'row')
Inputs may be any that keep to these rules, and one draw needn't show every extreme that they name: Each row of crop_tiles names 8 different tiles of the 16, in increasing order; its last 4 entries are the tiles 16 - 8 // 2 to 15.
All inputs are finite; a program needn't handle non-finite values.
Results may differ from a plain program's by a relative error of at most 0.014.
Values may be sent and summed in bfloat16 or wider, within the bound.
A program may use at most 256 MiB of HBM per device.

v0:
```python
import jax
import jax.numpy as jnp
from jax import lax
from jax.sharding import PartitionSpec as P

CH = 64
CROP = 1024
TILE = 128
NLAYER = 2
FULL = 2048


EPSILON = 1e-05


def from_partner(value, axis, bit):
    mask = 2**bit
    pairs = [(source, source ^ mask) for source in range(lax.axis_size(axis))]
    return lax.ppermute(value, axis, pairs)


def channel_norm(values):
    center = values - jnp.mean(values, axis=0, keepdims=True)
    spread = jnp.mean(center * center, axis=0, keepdims=True)
    return center * lax.rsqrt(spread + EPSILON)


def on_device(pair_maps, crop_tiles, full_length, proj_weight, out_weight, final_weight):
    row_count = lax.axis_size("row")
    my_index = lax.axis_index("row")
    pair_local = pair_maps[0]
    crop_ids = crop_tiles[0]
    local_rows = pair_local.shape[0]
    col_width = CROP // row_count
    parts_count = max(1, row_count // CH)
    per_group = CH * parts_count // row_count
    groups = CH // per_group
    part_rows = CROP // parts_count
    steps_crop = jnp.arange(CROP, dtype=jnp.int32)
    position = crop_ids[steps_crop // TILE] * TILE + steps_crop % TILE
    usable = (position < full_length[0]).astype(jnp.float32)
    col_usable = lax.dynamic_slice_in_dim(usable, my_index * col_width, col_width)
    pair_mask = col_usable[:, None] * usable[None, :]
    columns = pair_local.reshape(local_rows, FULL // TILE, TILE, CH)[:, crop_ids]
    columns = columns.reshape(local_rows, CROP * CH)
    received = lax.all_to_all(columns, "row", split_axis=1, concat_axis=0, tiled=True)
    cropped = received.reshape(FULL // TILE, TILE, col_width * CH)[crop_ids]
    current = jnp.transpose(cropped.reshape(CROP, col_width, CH), (2, 1, 0))
    for layer_idx in range(NLAYER):
        normed_in = channel_norm(current.astype(jnp.float32)).astype(jnp.bfloat16)
        projected = jnp.einsum(
            "cd,cwi->dwi", proj_weight[layer_idx], normed_in, preferred_element_type=jnp.float32
        )
        left_proj = (jax.nn.sigmoid(projected[:CH]) * projected[CH : 2 * CH] * pair_mask).astype(
            jnp.bfloat16
        )
        right_proj = (
            jax.nn.sigmoid(projected[2 * CH : 3 * CH]) * projected[3 * CH : 4 * CH] * pair_mask
        ).astype(jnp.bfloat16)
        gate_vals = jax.nn.sigmoid(projected[4 * CH :])
        left_send = left_proj.reshape(groups, per_group, col_width, parts_count, part_rows)
        left_send = jnp.transpose(left_send, (0, 3, 1, 2, 4)).reshape(
            row_count, per_group, col_width, part_rows
        )
        right_send = right_proj.reshape(groups, per_group, col_width, parts_count, part_rows)
        right_send = jnp.transpose(right_send, (0, 3, 1, 2, 4)).reshape(
            row_count, per_group, col_width, part_rows
        )
        left_got, right_got = (
            lax.all_to_all(left_send, "row", split_axis=0, concat_axis=2, tiled=True),
            lax.all_to_all(right_send, "row", split_axis=0, concat_axis=2, tiled=True),
        )
        right_whole = right_got[0]
        for bit_pos in range(parts_count.bit_length() - 1):
            partner = from_partner(right_whole, "row", bit_pos)
            lower_side = my_index // (1 << bit_pos) % 2 == 0
            right_whole = jnp.where(
                lower_side,
                jnp.concatenate([right_whole, partner], axis=2),
                jnp.concatenate([partner, right_whole], axis=2),
            )
        products = jnp.einsum(
            "cki,ckj->cij", left_got[0], right_whole, preferred_element_type=jnp.float32
        ).astype(jnp.bfloat16)
        back_send = jnp.transpose(
            products.reshape(per_group, part_rows, row_count, col_width), (2, 0, 3, 1)
        )
        back_got = lax.all_to_all(back_send, "row", split_axis=0, concat_axis=0, tiled=True)
        merged = back_got.reshape(groups, parts_count, per_group, col_width, part_rows)
        merged = jnp.transpose(merged, (0, 2, 3, 1, 4)).reshape(CH, col_width, CROP)
        normed_out = channel_norm(merged.astype(jnp.float32)).astype(jnp.bfloat16)
        update = jnp.einsum(
            "cd,cwi->dwi", out_weight[layer_idx], normed_out, preferred_element_type=jnp.float32
        )
        current = (current.astype(jnp.float32) + gate_vals * update).astype(jnp.bfloat16)
    normed_final = channel_norm(current.astype(jnp.float32))
    template_count = lax.axis_size("tmpl")
    summed = lax.psum(normed_final.astype(jnp.bfloat16), "tmpl").astype(jnp.float32)
    hidden = jnp.maximum(summed / template_count, 0.0).astype(jnp.bfloat16)
    result = jnp.einsum(
        "cz,cwi->zwi", final_weight, hidden, preferred_element_type=jnp.float32
    ).astype(jnp.bfloat16)
    return result


def solution(mesh):
    placed = (P("tmpl", "row", None, None), P("tmpl", None), P(), P(), P(), P())
    return jax.shard_map(
        on_device, mesh=mesh, in_specs=placed, out_specs=P(None, "row", None), check_vma=False
    )
```

profile of v0, /device:TPU:0, one launch (start us, length us, event | category | flops | bytes accessed | tf_op | source)
XLA Modules:
  0.0 2191.1 jit_solution(17895547793072402721)
XLA Ops:
  7.2 58.6 %copy.32 = bf16[1,128,2048,64]{3,2,1,0:T(8,128)(2,1)} copy(bf16[1,128,2048,64]{2,3,1,0:T(8,128)(2,1)} %param.6) | data formatting | bytes 67108864 | tf_op args[0]
  65.8 105.2 %while.1 = (s32[]{:T(128)}, bf16[128,16,128,64]{3,2,1,0:T(8,128)(2,1)}, s32[8,1]{0,1:T(1,128)S(1)}, bf16[8,128,128,64]{1,3,2,0:T(8,128)(2,1)}, s32[]{:T(128)}) while((s32[]{:T(128)}, bf16[128,16,128,64]{3,2,1,0:T(8,128)(2,1)}, s32[8,1]{0,1:T(1,128)S(1)}, bf16[8,128,128,64]{1,3,2,0:T(8,128)(2,1)}, s32[]{:T(128)}) %tuple.28), condition=%wide.while_cond, body=%wide.while_body.sunk | while | flops 2 | bytes 12583001 | solution.py:44
  171.0 20.8 copy.34
  207.0 308.7 %all-to-all-done = bf16[128,16,4096]{2,0,1:T(8,128)(2,1)} async-done(((bf16[128,16,4096]{2,0,1:T(8,128)(2,1)}), bf16[128,16,4096]{2,0,1:T(8,128)(2,1)}, u32[]{:S(2)}, u32[]{:S(2)}) %all-to-all-start) | async-done | bytes 16777248 | tf_op jit(solution)/shard_map/all_to_all | solution.py:46
  539.1 18.0 reshape.222
  575.0 34.1 %convolution_bitcast_fusion.1 = f32[320,64,1024]{2,0,1:T(8,128)} fusion(f32[1024,64,64]{0,2,1:T(8,128)} %reshape.222, f32[64,1024]{1,0:T(8,128)S(1)} %add_rsqrt_fusion.4, f32[64,1024]{1,0:T(8,128)S(1)} %broadcast_multiply_fusion.5, bf16[2,64,320]{2,1,0:T(8,128)(2,1)S(1)} %copy-done.4), kind=kOutput, calls=%fused_computation.5 | convolution fusion | flops 2696937472 | bytes 101236736 | tf_op jit(solution)/shard_map/cd,cwi->dwi/dot_general | solution.py:51
  609.1 29.9 %fusion.32 = (bf16[64,64,1024]{2,0,1:T(8,128)(2,1)}, bf16[64,64,1024]{2,0,1:T(8,128)(2,1)}) fusion(f32[320,64,1024]{2,0,1:T(8,128)} %convolution_bitcast_fusion.1, f32[64,1024]{1,0:T(8,128)S(1)} %broadcast_multiply_fusion), kind=kLoop, calls=%fused_computation.53 | loop fusion | flops 50331648 | bytes 84148224 | tf_op jit(solution)/shard_map/convert_element_type | solution.py:59
  660.1 73.2 %all-to-all-start.1 = ((bf16[16,4,64,1024]{3,1,2,0:T(4,128)(2,1)}), bf16[16,4,64,1024]{3,1,2,0:T(4,128)(2,1)}, u32[]{:S(2)}, u32[]{:S(2)}) async-start(bf16[16,4,64,1024]{3,1,2,0:T(4,128)(2,1)} %copy.36), calls=%async_computation.1 | async-start | bytes 16777216 | tf_op jit(solution)/shard_map/all_to_all | solution.py:70
  744.8 142.5 %all-to-all-done.1 = bf16[16,4,64,1024]{3,1,2,0:T(4,128)(2,1)} async-done(((bf16[16,4,64,1024]{3,1,2,0:T(4,128)(2,1)}), bf16[16,4,64,1024]{3,1,2,0:T(4,128)(2,1)}, u32[]{:S(2)}, u32[]{:S(2)}) %all-to-all-start.1) | async-done | bytes 8388640 | tf_op jit(solution)/shard_map/all_to_all | solution.py:70
  887.3 39.9 %all-to-all-start.2 = ((bf16[16,4,64,1024]{3,2,1,0:T(8,128)(2,1)}), bf16[16,4,64,1024]{3,2,1,0:T(8,128)(2,1)}, u32[]{:S(2)}, u32[]{:S(2)}) async-start(bf16[16,4,64,1024]{3,2,1,0:T(8,128)(2,1)} %bitcast.118), calls=%async_computation.2 | async-start | bytes 16777216 | tf_op jit(solution)/shard_map/all_to_all | solution.py:71
  936.8 141.5 %all-to-all-done.2 = bf16[16,4,64,1024]{3,2,1,0:T(8,128)(2,1)} async-done(((bf16[16,4,64,1024]{3,2,1,0:T(8,128)(2,1)}), bf16[16,4,64,1024]{3,2,1,0:T(8,128)(2,1)}, u32[]{:S(2)}, u32[]{:S(2)}) %all-to-all-start.2) | async-done | bytes 8388640 | tf_op jit(solution)/shard_map/all_to_all | solution.py:71
  1086.8 15.8 convolution_convert_fusion.1
  1111.2 219.8 %all_to_all.86 = bf16[16,4,64,1024]{3,2,1,0:T(8,128)(2,1)S(1)} all-to-all(bf16[16,4,64,1024]{3,2,1,0:T(8,128)(2,1)} %bitcast.119), channel_id=1, replica_groups=mesh['tmpl'=2,'row'=16] {'row'}, dimensions={0} | all-to-all | bytes 16777216 | tf_op jit(solution)/shard_map/all_to_all | solution.py:88
  1346.8 20.2 convert_reduce_fusion
  1374.2 31.9 %convolution_bitcast_fusion = f32[320,64,1024]{2,0,1:T(8,128)} fusion(bf16[64,64,1024]{2,0,1:T(8,128)(2,1)} %copy-done.3, f32[64,1024]{1,0:T(8,128)S(1)} %add_rsqrt_fusion.2, f32[64,1024]{1,0:T(8,128)S(1)} %broadcast_multiply_fusion.3, bf16[2,64,320]{2,1,0:T(8,128)(2,1)S(1)} %copy-done.4), kind=kOutput, calls=%fused_computation.4 | convolution fusion | flops 2701131776 | bytes 92848128 | tf_op jit(solution)/shard_map/cd,cwi->dwi/dot_general | solution.py:51
  1406.1 29.6 %fusion.18 = (bf16[64,64,1024]{2,0,1:T(8,128)(2,1)}, bf16[64,64,1024]{2,0,1:T(8,128)(2,1)}) fusion(f32[320,64,1024]{2,0,1:T(8,128)} %convolution_bitcast_fusion, f32[64,1024]{1,0:T(8,128)S(1)} %broadcast_multiply_fusion), kind=kLoop, calls=%fused_computation.34 | loop fusion | flops 50331648 | bytes 84148224 | tf_op jit(solution)/shard_map/convert_element_type | solution.py:59
  1473.4 141.2 %all-to-all-done.4 = bf16[16,4,64,1024]{3,1,2,0:T(4,128)(2,1)} async-done(((bf16[16,4,64,1024]{3,1,2,0:T(4,128)(2,1)}), bf16[16,4,64,1024]{3,1,2,0:T(4,128)(2,1)}, u32[]{:S(2)}, u32[]{:S(2)}) %all-to-all-start.4) | async-done | bytes 8388640 | tf_op jit(solution)/shard_map/all_to_all | solution.py:70
  1614.6 38.5 %all-to-all-start.5 = ((bf16[16,4,64,1024]{3,2,1,0:T(8,128)(2,1)}), bf16[16,4,64,1024]{3,2,1,0:T(8,128)(2,1)}, u32[]{:S(2)}, u32[]{:S(2)}) async-start(bf16[16,4,64,1024]{3,2,1,0:T(8,128)(2,1)} %bitcast.117), calls=%async_computation.5 | async-start | bytes 16777216 | tf_op jit(solution)/shard_map/all_to_all | solution.py:71
  1662.6 141.4 %all-to-all-done.5 = bf16[16,4,64,1024]{3,2,1,0:T(8,128)(2,1)} async-done(((bf16[16,4,64,1024]{3,2,1,0:T(8,128)(2,1)}), bf16[16,4,64,1024]{3,2,1,0:T(8,128)(2,1)}, u32[]{:S(2)}, u32[]{:S(2)}) %all-to-all-start.5) | async-done | bytes 8388640 | tf_op jit(solution)/shard_map/all_to_all | solution.py:71
  1812.4 16.4 convolution_convert_fusion
  1837.1 219.7 %all_to_all.87 = bf16[16,4,64,1024]{3,2,1,0:T(8,128)(2,1)S(1)} all-to-all(bf16[16,4,64,1024]{3,2,1,0:T(8,128)(2,1)} %bitcast.120), channel_id=1, replica_groups=mesh['tmpl'=2,'row'=16] {'row'}, dimensions={0} | all-to-all | bytes 16777216 | tf_op jit(solution)/shard_map/all_to_all | solution.py:88
  2072.4 23.5 %convert_reduce_fusion.1 = (f32[64,1024]{1,0:T(8,128)S(1)}, bf16[64,64,1024]{2,0,1:T(8,128)(2,1)}) fusion(bf16[64,64,1024]{2,1,0:T(8,128)(2,1)} %bitcast.125, bf16[2,64,64]{2,1,0:T(8,128)(2,1)S(1)} %copy-done.6, f32[320,64,1024]{2,0,1:T(8,128)} %convolution_bitcast_fusion, bf16[64,64,1024]{2,0,1:T(8,128)(2,1)} %copy-done.3), kind=kOutput, calls=%fused_computation.10 | convolution fusion | flops 574554112 | bytes 42221568 | tf_op jit(solution)/shard_map/cd,cwi->dwi/dot_general | solution.py:92
  2113.8 36.5 %all-reduce.2.cloned.1.call-done = bf16[64,64,1024]{2,0,1:T(8,128)(2,1)} async-done(((bf16[64,64,1024]{2,0,1:T(8,128)(2,1)}), bf16[64,64,1024]{2,0,1:T(8,128)(2,1)}) %all-reduce.2.cloned.1.call-update) | async-done | bytes 8388624 | tf_op jit(solution)/shard_map/psum | solution.py:98
  2160.6 23.3 %copy.52 = bf16[128,64,1024]{2,1,0:T(8,128)(2,1)} copy(bf16[128,64,1024]{0,2,1:T(8,128)(2,1)} %convert_bitcast_fusion) | data formatting | bytes 33554432 | tf_op jit(solution)/shard_map/convert_element_type | solution.py:102
  (95 shorter events, 351.6 us)
Async XLA Ops:
  6.5 2143.8 %copy-start = (bf16[64,128]{1,0:T(8,128)(2,1)S(1)}, bf16[64,128]{1,0:T(8,128)(2,1)}, u32[]{:S(2)}) copy-start(bf16[64,128]{1,0:T(8,128)(2,1)} %param.11) | copy-start | bytes 49156
  191.8 9.4 copy-start.5
  191.8 323.9 %all-to-all-start = ((bf16[128,16,4096]{2,0,1:T(8,128)(2,1)}), bf16[128,16,4096]{2,0,1:T(8,128)(2,1)}, u32[]{:S(2)}, u32[]{:S(2)}) async-start(bf16[128,16,4096]{2,0,1:T(8,128)(2,1)} %copy.34), calls=%async_computation | async-start | bytes 33554432 | tf_op jit(solution)/shard_map/all_to_all | solution.py:46
  557.1 18.0 copy-start.4
  660.1 227.2 %all-to-all-start.1 = ((bf16[16,4,64,1024]{3,1,2,0:T(4,128)(2,1)}), bf16[16,4,64,1024]{3,1,2,0:T(4,128)(2,1)}, u32[]{:S(2)}, u32[]{:S(2)}) async-start(bf16[16,4,64,1024]{3,1,2,0:T(4,128)(2,1)} %copy.36), calls=%async_computation.1 | async-start | bytes 16777216 | tf_op jit(solution)/shard_map/all_to_all | solution.py:70
  887.3 191.0 %all-to-all-start.2 = ((bf16[16,4,64,1024]{3,2,1,0:T(8,128)(2,1)}), bf16[16,4,64,1024]{3,2,1,0:T(8,128)(2,1)}, u32[]{:S(2)}, u32[]{:S(2)}) async-start(bf16[16,4,64,1024]{3,2,1,0:T(8,128)(2,1)} %bitcast.118), calls=%async_computation.2 | async-start | bytes 16777216 | tf_op jit(solution)/shard_map/all_to_all | solution.py:71
  1331.0 3.6 copy-start.1
  1331.0 15.8 copy-start.6
  1367.0 3.4 copy-start.3
  1456.9 157.7 %all-to-all-start.4 = ((bf16[16,4,64,1024]{3,1,2,0:T(4,128)(2,1)}), bf16[16,4,64,1024]{3,1,2,0:T(4,128)(2,1)}, u32[]{:S(2)}, u32[]{:S(2)}) async-start(bf16[16,4,64,1024]{3,1,2,0:T(4,128)(2,1)} %copy.44), calls=%async_computation.4 | async-start | bytes 16777216 | tf_op jit(solution)/shard_map/all_to_all | solution.py:70
  1614.6 189.3 %all-to-all-start.5 = ((bf16[16,4,64,1024]{3,2,1,0:T(8,128)(2,1)}), bf16[16,4,64,1024]{3,2,1,0:T(8,128)(2,1)}, u32[]{:S(2)}, u32[]{:S(2)}) async-start(bf16[16,4,64,1024]{3,2,1,0:T(8,128)(2,1)} %bitcast.117), calls=%async_computation.5 | async-start | bytes 16777216 | tf_op jit(solution)/shard_map/all_to_all | solution.py:71
  1653.1 497.2 %all-reduce.2.cloned.1.call-start = ((), (), s32[]{:S(2)}) async-start(), calls=%async_computation.7 | async-start | bytes 16777216 | tf_op jit(solution)/shard_map/psum | solution.py:98
  2056.8 3.7 copy-start.2
Sparse Core Ops, SparseCore 0:
  2114.0 36.3 all-reduce.1
where the time goes:
time: 2200 us; the launch traced here: 2190 us
  waiting for transfers between devices  912 us (41%)
  blocking collectives  439 us (20%)
  local copies, waits for them, and re-layouts  375 us (17%)
  starting transfers between devices  165 us (8%)
  matrix products  152 us (7%)
  other arithmetic  133 us (6%)
    all_to_all x2, blocking collectives, on_device(): lax.all_to_all(back_send, 'row', split_axis=0, concat_axis=0, tiled=True)  439 us
    all_to_all x1, waiting for transfers between devices, on_device(): lax.all_to_all(columns, 'row', split_axis=1, concat_axis=0, tiled=True)  309 us
    all_to_all x2, waiting for transfers between devices, on_device(): lax.all_to_all(left_send, 'row', split_axis=0, concat_axis=2, tiled=True)  284 us
    all_to_all x2, waiting for transfers between devices, on_device(): lax.all_to_all(right_send, 'row', split_axis=0, concat_axis=2, tiled=True)  283 us
    gather x32, local copies, waits for them, and re-layouts  105 us
    all_to_all x2, starting transfers between devices, on_device(): lax.all_to_all(right_send, 'row', split_axis=0, concat_axis=2, tiled=True)  78.3 us
    all_to_all x2, starting transfers between devices, on_device(): lax.all_to_all(left_send, 'row', split_axis=0, concat_axis=2, tiled=True)  78.3 us
    dot_general x2, matrix products, on_device(): jnp.einsum('cd,cwi->dwi', proj_weight[layer_idx], normed_in, preferred_el...  66 us
  transfers between devices with their start and end apart: 6, of which 6 were waited for; matrix products, arithmetic and copies ran while one was open for 2% of the time, Pallas kernels for 0%

commit v1 on v0

--- a/solution.py
+++ b/solution.py
@@ -1,6 +1,8 @@
 import jax
 import jax.numpy as jnp
 from jax import lax
+from jax.experimental import pallas as pl
+from jax.experimental.pallas import tpu as pltpu
 from jax.sharding import PartitionSpec as P
 
 CH = 64
@@ -23,6 +25,114 @@
     center = values - jnp.mean(values, axis=0, keepdims=True)
     spread = jnp.mean(center * center, axis=0, keepdims=True)
     return center * lax.rsqrt(spread + EPSILON)
+
+
+SPLIT = 2
+
+
+def product_kernel(left_ref, *refs):
+    rights, out_ref = refs[:-1], refs[-1]
+    sources, _, width, chunk = left_ref.shape
+    left = left_ref[...].reshape(sources * width, chunk)
+    per = out_ref.shape[0] // len(rights)
+    for number, right_ref in enumerate(rights):
+        right = right_ref[...].reshape(sources * width, right_ref.shape[-1])
+        product = lax.dot_general(
+            right, left, (((0,), (0,)), ((), ())), preferred_element_type=jnp.float32
+        )
+        out_ref[number * per : (number + 1) * per] = product.astype(out_ref.dtype).reshape(
+            per, 1, width, chunk
+        )
+
+
+def channel_products(left, rights):
+    sources, channels, width, chunk = left.shape
+    spec = pl.BlockSpec((sources, 1, width, chunk), lambda c: (0, c, 0, 0))
+    depth = sources * width
+    return pl.pallas_call(
+        product_kernel,
+        grid=(channels,),
+        in_specs=[spec] * (1 + len(rights)),
+        out_specs=spec,
+        out_shape=jax.ShapeDtypeStruct(left.shape, left.dtype),
+        compiler_params=pltpu.CompilerParams(vmem_limit_bytes=32 << 20),
+        cost_estimate=pl.CostEstimate(
+            flops=2 * channels * depth * depth * chunk,
+            bytes_accessed=2 * left.size * (2 + len(rights)),
+            transcendentals=0,
+        ),
+    )(left, *rights)
+
+
+def exchange(value):
+    return lax.all_to_all(value, "row", split_axis=0, concat_axis=0, tiled=True)
+
+
+def in_chunks(pair_maps, crop_tiles, full_length, proj_weight, out_weight, final_weight):
+    row_count = lax.axis_size("row")
+    my_index = lax.axis_index("row")
+    crop_ids = crop_tiles[0]
+    col_width = CROP // row_count
+    per_group = CH // row_count
+    tiles = CROP // TILE
+    chunk = CROP // SPLIT
+    steps_crop = jnp.arange(CROP, dtype=jnp.int32)
+    position = crop_ids[steps_crop // TILE] * TILE + steps_crop % TILE
+    usable = (position < full_length[0]).astype(jnp.float32)
+    col_usable = lax.dynamic_slice_in_dim(usable, my_index * col_width, col_width)
+    pair_mask = col_usable[:, None] * usable[None, :]
+    masks = jnp.split(pair_mask, SPLIT, axis=1)
+    by_channel = jnp.transpose(pair_maps[0], (0, 2, 1))
+    columns = jnp.concatenate(
+        [
+            lax.dynamic_slice_in_dim(by_channel, crop_ids[tile] * TILE, TILE, axis=2)
+            for tile in range(tiles)
+        ],
+        axis=2,
+    )
+    send = jnp.transpose(columns, (2, 1, 0)).reshape(row_count, col_width, CH, TILE)
+    got = exchange(send)
+    per = tiles // SPLIT
+    current = []
+    for number in range(SPLIT):
+        pieces = [
+            lax.dynamic_index_in_dim(got, crop_ids[number * per + tile], 0, keepdims=False)
+            for tile in range(per)
+        ]
+        current.append(jnp.transpose(jnp.concatenate(pieces, axis=2), (1, 0, 2)))
+    for layer_idx in range(NLAYER):
+        lefts, rights, gates = [], [], []
+        for values, mask in zip(current, masks):
+            normed_in = channel_norm(values.astype(jnp.float32)).astype(jnp.bfloat16)
+            projected = jnp.einsum(
+                "cd,cwi->dwi", proj_weight[layer_idx], normed_in, preferred_element_type=jnp.float32
+            )
+            left = jax.nn.sigmoid(projected[:CH]) * projected[CH : 2 * CH] * mask
+            right = jax.nn.sigmoid(projected[2 * CH : 3 * CH]) * projected[3 * CH : 4 * CH] * mask
+            shape = (row_count, per_group, col_width, chunk)
+            rights.append(exchange(right.astype(jnp.bfloat16).reshape(shape)))
+            lefts.append(exchange(left.astype(jnp.bfloat16).reshape(shape)))
+            gates.append(jax.nn.sigmoid(projected[4 * CH :]))
+        following = []
+        for values, left, gate in zip(current, lefts, gates):
+            merged = exchange(channel_products(left, rights)).reshape(CH, col_width, chunk)
+            normed_out = channel_norm(merged.astype(jnp.float32)).astype(jnp.bfloat16)
+            update = jnp.einsum(
+                "cd,cwi->dwi", out_weight[layer_idx], normed_out, preferred_element_type=jnp.float32
+            )
+            following.append((values.astype(jnp.float32) + gate * update).astype(jnp.bfloat16))
+        current = following
+    template_count = lax.axis_size("tmpl")
+    results = []
+    for values in current:
+        normed_final = channel_norm(values.astype(jnp.float32))
+        summed = lax.psum(normed_final.astype(jnp.bfloat16), "tmpl").astype(jnp.float32)
+        hidden = jnp.maximum(summed / template_count, 0.0).astype(jnp.bfloat16)
+        results.append(
+            jnp.einsum("cz,cwi->zwi", final_weight, hidden, preferred_element_type=jnp.float32)
+            .astype(jnp.bfloat16)
+        )
+    return jnp.concatenate(results, axis=2)
 
 
 def on_device(pair_maps, crop_tiles, full_length, proj_weight, out_weight, final_weight):
@@ -105,6 +215,12 @@
 
 def solution(mesh):
     placed = (P("tmpl", "row", None, None), P("tmpl", None), P(), P(), P(), P())
+    rows = mesh.shape["row"]
+    whole_tiles = FULL // rows == TILE and CH % rows == 0
     return jax.shard_map(
-        on_device, mesh=mesh, in_specs=placed, out_specs=P(None, "row", None), check_vma=False
+        in_chunks if whole_tiles else on_device,
+        mesh=mesh,
+        in_specs=placed,
+        out_specs=P(None, "row", None),
+        check_vma=False,
     )

time: 2200 us -> 1790 us (0.81)
  blocking collectives: 439 us -> 0 us
  local copies, waits for them, and re-layouts: 375 us -> 138 us
  starting transfers between devices: 165 us -> 297 us
  waiting for transfers between devices: 912 us -> 1030 us
  matrix products: 152 us -> 115 us
  Pallas kernels: 0 us -> 31.7 us
    all_to_all x2 -> x0, blocking collectives: 439 us -> none  [on_device(): lax.all_to_all(back_send, 'row', split_axis=0, concat_axis=0, tiled=True)]
    all_to_all x5 -> x13, starting transfers between devices: 165 us -> 297 us  [exchange(): return lax.all_to_all(value, 'row', split_axis=0, concat_axis=0, tiled=True)]
    gather x34 -> x0, local copies, waits for them, and re-layouts: 116 us -> none
    all_to_all x5 -> x13, waiting for transfers between devices: 875 us -> 978 us  [exchange(): return lax.all_to_all(value, 'row', split_axis=0, concat_axis=0, tiled=True)]
    another operation x6 -> x0, local copies, waits for them, and re-layouts: 65.1 us -> none  [the longest x4 42.4 us: on_device(): jnp.transpose(left_send, (0, 3, 1, 2, 4))]
    all_to_all x5 -> x0, local copies, waits for them, and re-layouts: 56.8 us -> none  [the longest x1 20.8 us: on_device(): lax.all_to_all(columns, 'row', split_axis=1, concat_axis=0, tiled=True)]
    dot_general x7 -> x10, matrix products: 152 us -> 115 us  [the longest x4 67.7 us: in_chunks(): jnp.einsum('cd,cwi->dwi', proj_weight[layer_idx], normed_in, preferred_el...]
    unnamed x15 -> x59, local copies, waits for them, and re-layouts: 65.1 us -> 30.4 us
  transfers between devices with their start and end apart: 6 -> 14, of which waited for: 6 -> 14; matrix products, arithmetic and copies ran while one was open for 2% -> 12% of each run, Pallas kernels for 0% -> 2%
where the time goes in v1:
time: 1790 us
  waiting for transfers between devices  1030 us (58%)
  starting transfers between devices  297 us (17%)
  other arithmetic  142 us (8%)
  local copies, waits for them, and re-layouts  138 us (8%)
  matrix products  115 us (6%)
  between operations  33.9 us (2%)
  Pallas kernels  31.7 us (2%)
    all_to_all x13, waiting for transfers between devices, exchange(): return lax.all_to_all(value, 'row', split_axis=0, concat_axis=0, tiled=True)  978 us
    all_to_all x13, starting transfers between devices, exchange(): return lax.all_to_all(value, 'row', split_axis=0, concat_axis=0, tiled=True)  297 us
    dot_general x4, matrix products, in_chunks(): jnp.einsum('cd,cwi->dwi', proj_weight[layer_idx], normed_in, preferred_el...  67.7 us
    psum x1, waiting for transfers between devices, in_chunks(): lax.psum(normed_final.astype(jnp.bfloat16), 'tmpl').astype(jnp.float32)  51.8 us
    dot_general x4, matrix products, in_chunks(): jnp.einsum('cd,cwi->dwi', out_weight[layer_idx], normed_out, preferred_el...  40.2 us
  transfers between devices with their start and end apart: 14, of which 14 were waited for; matrix products, arithmetic and copies ran while one was open for 12% of the time, Pallas kernels for 2%

profile of v1, /device:TPU:0, one launch (start us, length us, event | category | flops | bytes accessed | tf_op | source)
XLA Modules:
  0.0 1788.0 jit_solution(6446459816706652474)
XLA Ops:
  37.5 26.0 %copy.45 = bf16[1024,64,128]{2,1,0:T(8,128)(2,1)} copy(bf16[1024,64,128]{0,1,2:T(8,128)(2,1)} %bitcast.24) | data formatting | bytes 33554432 | tf_op jit(solution)/shard_map/transpose | solution.py:93
  92.4 294.9 %all-to-all-done = bf16[16,64,64,128]{3,2,1,0:T(8,128)(2,1)} async-done(((bf16[16,64,64,128]{3,2,1,0:T(8,128)(2,1)}), bf16[16,64,64,128]{3,2,1,0:T(8,128)(2,1)}, u32[]{:S(2)}, u32[]{:S(2)}) %all-to-all-start) | async-done | bytes 16777248 | tf_op jit(solution)/shard_map/all_to_all | solution.py:68
  436.9 73.4 %all-to-all-start.3 = ((bf16[16,4,64,512]{3,2,1,0:T(8,128)(2,1)}), bf16[16,4,64,512]{3,2,1,0:T(8,128)(2,1)}, u32[]{:S(2)}, u32[]{:S(2)}) async-start(bf16[16,4,64,512]{3,2,1,0:T(8,128)(2,1)} %bitcast.171), calls=%async_computation.3 | async-start | bytes 8388608 | tf_op jit(solution)/shard_map/all_to_all | solution.py:68
  551.0 37.7 %all-to-all-done.3.refs_1_ = bf16[16,4,64,512]{3,2,1,0:T(8,128)(2,1)} async-done(((bf16[16,4,64,512]{3,2,1,0:T(8,128)(2,1)}), bf16[16,4,64,512]{3,2,1,0:T(8,128)(2,1)}, u32[]{:S(2)}, u32[]{:S(2)}) %all-to-all-start.3) | async-done | bytes 4194336 | tf_op jit(solution)/shard_map/all_to_all | solution.py:68
  614.5 71.9 %all-to-all-done.1.left_ref = bf16[16,4,64,512]{3,2,1,0:T(8,128)(2,1)} async-done(((bf16[16,4,64,512]{3,2,1,0:T(8,128)(2,1)}), bf16[16,4,64,512]{3,2,1,0:T(8,128)(2,1)}, u32[]{:S(2)}, u32[]{:S(2)}) %all-to-all-start.1) | async-done | bytes 4194336 | tf_op jit(solution)/shard_map/all_to_all | solution.py:68
  686.5 19.4 %all-to-all-start.2 = ((bf16[16,4,64,512]{3,2,1,0:T(8,128)(2,1)}), bf16[16,4,64,512]{3,2,1,0:T(8,128)(2,1)}, u32[]{:S(2)}, u32[]{:S(2)}) async-start(bf16[16,4,64,512]{3,2,1,0:T(8,128)(2,1)} %bitcast.173), calls=%async_computation.2 | async-start | bytes 8388608 | tf_op jit(solution)/shard_map/all_to_all | solution.py:68
  712.5 71.9 %all-to-all-done.2.refs_0_ = bf16[16,4,64,512]{3,2,1,0:T(8,128)(2,1)} async-done(((bf16[16,4,64,512]{3,2,1,0:T(8,128)(2,1)}), bf16[16,4,64,512]{3,2,1,0:T(8,128)(2,1)}, u32[]{:S(2)}, u32[]{:S(2)}) %all-to-all-start.2) | async-done | bytes 4194336 | tf_op jit(solution)/shard_map/all_to_all | solution.py:68
  784.4 19.5 %all-to-all-start.7 = ((bf16[16,4,64,512]{3,2,1,0:T(8,128)(2,1)}), bf16[16,4,64,512]{3,2,1,0:T(8,128)(2,1)}, u32[]{:S(2)}, u32[]{:S(2)}) async-start(bf16[16,4,64,512]{3,2,1,0:T(8,128)(2,1)} %bitcast.175), calls=%async_computation.7 | async-start | bytes 8388608 | tf_op jit(solution)/shard_map/all_to_all | solution.py:68
  813.8 68.6 %all-to-all-done.7.left_ref = bf16[16,4,64,512]{3,2,1,0:T(8,128)(2,1)} async-done(((bf16[16,4,64,512]{3,2,1,0:T(8,128)(2,1)}), bf16[16,4,64,512]{3,2,1,0:T(8,128)(2,1)}, u32[]{:S(2)}, u32[]{:S(2)}) %all-to-all-start.7) | async-done | bytes 4194336 | tf_op jit(solution)/shard_map/all_to_all | solution.py:68
  882.3 19.5 %all-to-all-start.4 = ((bf16[16,4,64,512]{3,2,1,0:T(8,128)(2,1)}), bf16[16,4,64,512]{3,2,1,0:T(8,128)(2,1)}, u32[]{:S(2)}, u32[]{:S(2)}) async-start(bf16[16,4,64,512]{3,2,1,0:T(8,128)(2,1)} %copy-done.3), calls=%async_computation.4 | async-start | bytes 8388608 | tf_op jit(solution)/shard_map/all_to_all | solution.py:68
  911.8 68.5 %all-to-all-done.4 = bf16[16,4,64,512]{3,2,1,0:T(8,128)(2,1)} async-done(((bf16[16,4,64,512]{3,2,1,0:T(8,128)(2,1)}), bf16[16,4,64,512]{3,2,1,0:T(8,128)(2,1)}, u32[]{:S(2)}, u32[]{:S(2)}) %all-to-all-start.4) | async-done | bytes 4194336 | tf_op jit(solution)/shard_map/all_to_all | solution.py:68
  980.3 19.7 %all-to-all-start.8 = ((bf16[16,4,64,512]{3,2,1,0:T(8,128)(2,1)}), bf16[16,4,64,512]{3,2,1,0:T(8,128)(2,1)}, u32[]{:S(2)}, u32[]{:S(2)}) async-start(bf16[16,4,64,512]{3,2,1,0:T(8,128)(2,1)} %copy-done.1), calls=%async_computation.8 | async-start | bytes 8388608 | tf_op jit(solution)/shard_map/all_to_all | solution.py:68
  1116.1 60.1 %all-to-all-done.5.left_ref = bf16[16,4,64,512]{3,2,1,0:T(8,128)(2,1)} async-done(((bf16[16,4,64,512]{3,2,1,0:T(8,128)(2,1)}), bf16[16,4,64,512]{3,2,1,0:T(8,128)(2,1)}, u32[]{:S(2)}, u32[]{:S(2)}) %all-to-all-start.5) | async-done | bytes 4194336 | tf_op jit(solution)/shard_map/all_to_all | solution.py:68
  1176.3 19.9 %all-to-all-start.6 = ((bf16[16,4,64,512]{3,2,1,0:T(8,128)(2,1)}), bf16[16,4,64,512]{3,2,1,0:T(8,128)(2,1)}, u32[]{:S(2)}, u32[]{:S(2)}) async-start(bf16[16,4,64,512]{3,2,1,0:T(8,128)(2,1)} %bitcast.169), calls=%async_computation.6 | async-start | bytes 8388608 | tf_op jit(solution)/shard_map/all_to_all | solution.py:68
  1249.0 25.6 %all-to-all-done.6.refs_0_ = bf16[16,4,64,512]{3,2,1,0:T(8,128)(2,1)} async-done(((bf16[16,4,64,512]{3,2,1,0:T(8,128)(2,1)}), bf16[16,4,64,512]{3,2,1,0:T(8,128)(2,1)}, u32[]{:S(2)}, u32[]{:S(2)}) %all-to-all-start.6) | async-done | bytes 4194336 | tf_op jit(solution)/shard_map/all_to_all | solution.py:68
  1300.6 71.9 %all-to-all-done.9.refs_1_ = bf16[16,4,64,512]{3,2,1,0:T(8,128)(2,1)} async-done(((bf16[16,4,64,512]{3,2,1,0:T(8,128)(2,1)}), bf16[16,4,64,512]{3,2,1,0:T(8,128)(2,1)}, u32[]{:S(2)}, u32[]{:S(2)}) %all-to-all-start.9) | async-done | bytes 4194336 | tf_op jit(solution)/shard_map/all_to_all | solution.py:68
  1372.5 19.5 %all-to-all-start.11 = ((bf16[16,4,64,512]{3,2,1,0:T(8,128)(2,1)}), bf16[16,4,64,512]{3,2,1,0:T(8,128)(2,1)}, u32[]{:S(2)}, u32[]{:S(2)}) async-start(bf16[16,4,64,512]{3,2,1,0:T(8,128)(2,1)} %bitcast.176), calls=%async_computation.11 | async-start | bytes 8388608 | tf_op jit(solution)/shard_map/all_to_all | solution.py:68
  1401.9 68.6 %all-to-all-done.11.left_ref = bf16[16,4,64,512]{3,2,1,0:T(8,128)(2,1)} async-done(((bf16[16,4,64,512]{3,2,1,0:T(8,128)(2,1)}), bf16[16,4,64,512]{3,2,1,0:T(8,128)(2,1)}, u32[]{:S(2)}, u32[]{:S(2)}) %all-to-all-start.11) | async-done | bytes 4194336 | tf_op jit(solution)/shard_map/all_to_all | solution.py:68
  1470.5 19.5 %all-to-all-start.10 = ((bf16[16,4,64,512]{3,2,1,0:T(8,128)(2,1)}), bf16[16,4,64,512]{3,2,1,0:T(8,128)(2,1)}, u32[]{:S(2)}, u32[]{:S(2)}) async-start(bf16[16,4,64,512]{3,2,1,0:T(8,128)(2,1)} %copy-done.4), calls=%async_computation.10 | async-start | bytes 8388608 | tf_op jit(solution)/shard_map/all_to_all | solution.py:68
  1499.9 68.5 %all-to-all-done.10 = bf16[16,4,64,512]{3,2,1,0:T(8,128)(2,1)} async-done(((bf16[16,4,64,512]{3,2,1,0:T(8,128)(2,1)}), bf16[16,4,64,512]{3,2,1,0:T(8,128)(2,1)}, u32[]{:S(2)}, u32[]{:S(2)}) %all-to-all-start.10) | async-done | bytes 4194336 | tf_op jit(solution)/shard_map/all_to_all | solution.py:68
  1568.4 19.5 %all-to-all-start.12 = ((bf16[16,4,64,512]{3,2,1,0:T(8,128)(2,1)}), bf16[16,4,64,512]{3,2,1,0:T(8,128)(2,1)}, u32[]{:S(2)}, u32[]{:S(2)}) async-start(bf16[16,4,64,512]{3,2,1,0:T(8,128)(2,1)} %copy-done.2), calls=%async_computation.12 | async-start | bytes 8388608 | tf_op jit(solution)/shard_map/all_to_all | solution.py:68
  1613.3 53.1 %all-to-all-done.12 = bf16[16,4,64,512]{3,2,1,0:T(8,128)(2,1)} async-done(((bf16[16,4,64,512]{3,2,1,0:T(8,128)(2,1)}), bf16[16,4,64,512]{3,2,1,0:T(8,128)(2,1)}, u32[]{:S(2)}, u32[]{:S(2)}) %all-to-all-start.12) | async-done | bytes 4194336 | tf_op jit(solution)/shard_map/all_to_all | solution.py:68
  1691.8 51.8 %all-reduce.3.cloned.1.call-done = (bf16[64,64,512]{2,0,1:T(8,128)(2,1)}, bf16[64,64,512]{2,0,1:T(8,128)(2,1)}) async-done(((bf16[64,64,512]{2,0,1:T(8,128)(2,1)}, bf16[64,64,512]{2,0,1:T(8,128)(2,1)}), (bf16[64,64,512]{2,0,1:T(8,128)(2,1)}, bf16[64,64,512]{2,0,1:T(8,128)(2,1)})) %all-reduce.3.cloned.1.call-update) | async-done | bytes 8388624 | tf_op jit(solution)/shard_map/psum | solution.py:129
  1757.6 23.3 %copy.60 = bf16[128,64,1024]{2,1,0:T(8,128)(2,1)} copy(bf16[128,64,1024]{0,2,1:T(8,128)(2,1)} %pad_maximum_fusion) | data formatting | bytes 33554432 | tf_op jit(solution)/shard_map/concatenate | solution.py:135
  (143 shorter events, 461.9 us)
Async XLA Ops:
  6.5 1737.1 %copy-start = (bf16[64,128]{1,0:T(8,128)(2,1)S(1)}, bf16[64,128]{1,0:T(8,128)(2,1)}, u32[]{:S(2)}) copy-start(bf16[64,128]{1,0:T(8,128)(2,1)} %param.11) | copy-start | bytes 49156
  63.5 323.8 %all-to-all-start = ((bf16[16,64,64,128]{3,2,1,0:T(8,128)(2,1)}), bf16[16,64,64,128]{3,2,1,0:T(8,128)(2,1)}, u32[]{:S(2)}, u32[]{:S(2)}) async-start(bf16[16,64,64,128]{3,2,1,0:T(8,128)(2,1)} %bitcast.168), calls=%async_computation | async-start | bytes 33554432 | tf_op jit(solution)/shard_map/all_to_all | solution.py:68
  92.4 324.4 %copy-start.20 = (f32[64,512]{1,0:T(8,128)}, f32[64,512]{1,0:T(8,128)S(1)}, u32[]{:S(2)}) copy-start(f32[64,512]{1,0:T(8,128)S(1)} %get-tuple-element.24) | copy-start | bytes 393220
  392.7 24.0 %copy-start.9 = (bf16[64,64,128]{2,1,0:T(8,128)(2,1)}, bf16[64,64,128]{2,1,0:T(8,128)(2,1)S(1)}, u32[]{:S(2)}) copy-start(bf16[64,64,128]{2,1,0:T(8,128)(2,1)S(1)} %get-tuple-element.16) | copy-start | bytes 3145732
  392.7 24.0 %copy-start.11 = (bf16[64,64,128]{2,1,0:T(8,128)(2,1)}, bf16[64,64,128]{2,1,0:T(8,128)(2,1)S(1)}, u32[]{:S(2)}) copy-start(bf16[64,64,128]{2,1,0:T(8,128)(2,1)S(1)} %get-tuple-element.17) | copy-start | bytes 3145732
  392.8 24.0 %copy-start.13 = (bf16[64,64,128]{2,1,0:T(8,128)(2,1)}, bf16[64,64,128]{2,1,0:T(8,128)(2,1)S(1)}, u32[]{:S(2)}) copy-start(bf16[64,64,128]{2,1,0:T(8,128)(2,1)S(1)} %get-tuple-element.18) | copy-start | bytes 3145732
  392.8 24.0 %copy-start.14 = (bf16[64,64,128]{2,1,0:T(8,128)(2,1)}, bf16[64,64,128]{2,1,0:T(8,128)(2,1)S(1)}, u32[]{:S(2)}) copy-start(bf16[64,64,128]{2,1,0:T(8,128)(2,1)S(1)} %get-tuple-element.19) | copy-start | bytes 3145732
  432.5 77.7 %copy-start.23 = (f32[64,512]{1,0:T(8,128)S(1)}, f32[64,512]{1,0:T(8,128)}, u32[]{:S(2)}) copy-start(f32[64,512]{1,0:T(8,128)} %get-tuple-element.42) | copy-start | bytes 393220
  436.9 76.5 %copy-start.24 = (bf16[2,64,320]{2,1,0:T(8,128)(2,1)S(1)}, bf16[2,64,320]{2,1,0:T(8,128)(2,1)}, u32[]{:S(2)}) copy-start(bf16[2,64,320]{2,1,0:T(8,128)(2,1)} %param.9) | copy-start | bytes 245764
  436.9 151.8 %all-to-all-start.3 = ((bf16[16,4,64,512]{3,2,1,0:T(8,128)(2,1)}), bf16[16,4,64,512]{3,2,1,0:T(8,128)(2,1)}, u32[]{:S(2)}, u32[]{:S(2)}) async-start(bf16[16,4,64,512]{3,2,1,0:T(8,128)(2,1)} %bitcast.171), calls=%async_computation.3 | async-start | bytes 8388608 | tf_op jit(solution)/shard_map/all_to_all | solution.py:68
  588.7 97.8 %all-to-all-start.1 = ((bf16[16,4,64,512]{3,2,1,0:T(8,128)(2,1)}), bf16[16,4,64,512]{3,2,1,0:T(8,128)(2,1)}, u32[]{:S(2)}, u32[]{:S(2)}) async-start(bf16[16,4,64,512]{3,2,1,0:T(8,128)(2,1)} %bitcast.172), calls=%async_computation.1 | async-start | bytes 8388608 | tf_op jit(solution)/shard_map/all_to_all | solution.py:68
  686.5 97.9 %all-to-all-start.2 = ((bf16[16,4,64,512]{3,2,1,0:T(8,128)(2,1)}), bf16[16,4,64,512]{3,2,1,0:T(8,128)(2,1)}, u32[]{:S(2)}, u32[]{:S(2)}) async-start(bf16[16,4,64,512]{3,2,1,0:T(8,128)(2,1)} %bitcast.173), calls=%async_computation.2 | async-start | bytes 8388608 | tf_op jit(solution)/shard_map/all_to_all | solution.py:68
  784.4 98.0 %all-to-all-start.7 = ((bf16[16,4,64,512]{3,2,1,0:T(8,128)(2,1)}), bf16[16,4,64,512]{3,2,1,0:T(8,128)(2,1)}, u32[]{:S(2)}, u32[]{:S(2)}) async-start(bf16[16,4,64,512]{3,2,1,0:T(8,128)(2,1)} %bitcast.175), calls=%async_computation.7 | async-start | bytes 8388608 | tf_op jit(solution)/shard_map/all_to_all | solution.py:68
  882.3 97.9 %all-to-all-start.4 = ((bf16[16,4,64,512]{3,2,1,0:T(8,128)(2,1)}), bf16[16,4,64,512]{3,2,1,0:T(8,128)(2,1)}, u32[]{:S(2)}, u32[]{:S(2)}) async-start(bf16[16,4,64,512]{3,2,1,0:T(8,128)(2,1)} %copy-done.3), calls=%async_computation.4 | async-start | bytes 8388608 | tf_op jit(solution)/shard_map/all_to_all | solution.py:68
  980.3 98.1 %all-to-all-start.8 = ((bf16[16,4,64,512]{3,2,1,0:T(8,128)(2,1)}), bf16[16,4,64,512]{3,2,1,0:T(8,128)(2,1)}, u32[]{:S(2)}, u32[]{:S(2)}) async-start(bf16[16,4,64,512]{3,2,1,0:T(8,128)(2,1)} %copy-done.1), calls=%async_computation.8 | async-start | bytes 8388608 | tf_op jit(solution)/shard_map/all_to_all | solution.py:68
  1078.4 97.9 %all-to-all-start.5 = ((bf16[16,4,64,512]{3,2,1,0:T(8,128)(2,1)}), bf16[16,4,64,512]{3,2,1,0:T(8,128)(2,1)}, u32[]{:S(2)}, u32[]{:S(2)}) async-start(bf16[16,4,64,512]{3,2,1,0:T(8,128)(2,1)} %bitcast.170), calls=%async_computation.5 | async-start | bytes 8388608 | tf_op jit(solution)/shard_map/all_to_all | solution.py:68
  1110.5 85.7 %copy-start.10 = (bf16[64,64,128]{2,1,0:T(8,128)(2,1)S(1)}, bf16[64,64,128]{2,1,0:T(8,128)(2,1)}, u32[]{:S(2)}) copy-start(bf16[64,64,128]{2,1,0:T(8,128)(2,1)} %copy-done.9) | copy-start | bytes 3145732
  1110.5 85.7 %copy-start.12 = (bf16[64,64,128]{2,1,0:T(8,128)(2,1)S(1)}, bf16[64,64,128]{2,1,0:T(8,128)(2,1)}, u32[]{:S(2)}) copy-start(bf16[64,64,128]{2,1,0:T(8,128)(2,1)} %copy-done.11) | copy-start | bytes 3145732
  1176.3 98.3 %all-to-all-start.6 = ((bf16[16,4,64,512]{3,2,1,0:T(8,128)(2,1)}), bf16[16,4,64,512]{3,2,1,0:T(8,128)(2,1)}, u32[]{:S(2)}, u32[]{:S(2)}) async-start(bf16[16,4,64,512]{3,2,1,0:T(8,128)(2,1)} %bitcast.169), calls=%async_computation.6 | async-start | bytes 8388608 | tf_op jit(solution)/shard_map/all_to_all | solution.py:68
  1274.6 97.9 %all-to-all-start.9 = ((bf16[16,4,64,512]{3,2,1,0:T(8,128)(2,1)}), bf16[16,4,64,512]{3,2,1,0:T(8,128)(2,1)}, u32[]{:S(2)}, u32[]{:S(2)}) async-start(bf16[16,4,64,512]{3,2,1,0:T(8,128)(2,1)} %bitcast.174), calls=%async_computation.9 | async-start | bytes 8388608 | tf_op jit(solution)/shard_map/all_to_all | solution.py:68
  1372.5 98.0 %all-to-all-start.11 = ((bf16[16,4,64,512]{3,2,1,0:T(8,128)(2,1)}), bf16[16,4,64,512]{3,2,1,0:T(8,128)(2,1)}, u32[]{:S(2)}, u32[]{:S(2)}) async-start(bf16[16,4,64,512]{3,2,1,0:T(8,128)(2,1)} %bitcast.176), calls=%async_computation.11 | async-start | bytes 8388608 | tf_op jit(solution)/shard_map/all_to_all | solution.py:68
  1470.5 97.9 %all-to-all-start.10 = ((bf16[16,4,64,512]{3,2,1,0:T(8,128)(2,1)}), bf16[16,4,64,512]{3,2,1,0:T(8,128)(2,1)}, u32[]{:S(2)}, u32[]{:S(2)}) async-start(bf16[16,4,64,512]{3,2,1,0:T(8,128)(2,1)} %copy-done.4), calls=%async_computation.10 | async-start | bytes 8388608 | tf_op jit(solution)/shard_map/all_to_all | solution.py:68
  1568.4 97.9 %all-to-all-start.12 = ((bf16[16,4,64,512]{3,2,1,0:T(8,128)(2,1)}), bf16[16,4,64,512]{3,2,1,0:T(8,128)(2,1)}, u32[]{:S(2)}, u32[]{:S(2)}) async-start(bf16[16,4,64,512]{3,2,1,0:T(8,128)(2,1)} %copy-done.2), calls=%async_computation.12 | async-start | bytes 8388608 | tf_op jit(solution)/shard_map/all_to_all | solution.py:68
  1587.9 155.7 %all-reduce.3.cloned.1.call-start = ((), (), s32[]{:S(2)}) async-start(), calls=%async_computation.13 | async-start | bytes 16777216 | tf_op jit(solution)/shard_map/psum | solution.py:129
  (16 other events, 137.1 us)
Sparse Core Ops, SparseCore 0:
  1692.0 51.5 all-reduce.2

commit v2 on v1

--- a/solution.py
+++ b/solution.py
@@ -66,6 +66,17 @@
 
 def exchange(value):
     return lax.all_to_all(value, "row", split_axis=0, concat_axis=0, tiled=True)
+
+
+def template_sum(values):
+    template_count = lax.axis_size("tmpl")
+    passing = channel_norm(values.astype(jnp.float32)).astype(jnp.bfloat16)
+    terms = [passing]
+    for _ in range(template_count - 1):
+        ring = [(source, (source + 1) % template_count) for source in range(template_count)]
+        passing = lax.ppermute(passing, "tmpl", ring)
+        terms.append(passing)
+    return sum(term.astype(jnp.float32) for term in terms)
 
 
 def in_chunks(pair_maps, crop_tiles, full_length, proj_weight, out_weight, final_weight):
@@ -113,21 +124,23 @@
             rights.append(exchange(right.astype(jnp.bfloat16).reshape(shape)))
             lefts.append(exchange(left.astype(jnp.bfloat16).reshape(shape)))
             gates.append(jax.nn.sigmoid(projected[4 * CH :]))
-        following = []
+        following, summed = [], []
         for values, left, gate in zip(current, lefts, gates):
             merged = exchange(channel_products(left, rights)).reshape(CH, col_width, chunk)
+            if summed:
+                merged, summed[-1] = lax.optimization_barrier((merged, summed[-1]))
             normed_out = channel_norm(merged.astype(jnp.float32)).astype(jnp.bfloat16)
             update = jnp.einsum(
                 "cd,cwi->dwi", out_weight[layer_idx], normed_out, preferred_element_type=jnp.float32
             )
             following.append((values.astype(jnp.float32) + gate * update).astype(jnp.bfloat16))
+            if layer_idx == NLAYER - 1:
+                summed.append(template_sum(following[-1]))
         current = following
     template_count = lax.axis_size("tmpl")
     results = []
-    for values in current:
-        normed_final = channel_norm(values.astype(jnp.float32))
-        summed = lax.psum(normed_final.astype(jnp.bfloat16), "tmpl").astype(jnp.float32)
-        hidden = jnp.maximum(summed / template_count, 0.0).astype(jnp.bfloat16)
+    for total in summed:
+        hidden = jnp.maximum(total / template_count, 0.0).astype(jnp.bfloat16)
         results.append(
             jnp.einsum("cz,cwi->zwi", final_weight, hidden, preferred_element_type=jnp.float32)
             .astype(jnp.bfloat16)

time: 1790 us -> 1820 us (1.017); the launches traced: 1790 us -> 1790 us
    psum x1 -> x0, waiting for transfers between devices: 51.8 us -> none  [in_chunks(): lax.psum(normed_final.astype(jnp.bfloat16), 'tmpl').astype(jnp.float32)]
    all_to_all x13, waiting for transfers between devices: 978 us -> 1030 us  [exchange(): return lax.all_to_all(value, 'row', split_axis=0, concat_axis=0, tiled=True)]
  transfers between devices with their start and end apart: 14 -> 15, of which waited for: 14 -> 15; matrix products, arithmetic and copies ran while one was open for 12% -> 9% of each run, Pallas kernels for 2% -> 2%
where the time goes in v2:
time: 1820 us; the launch traced here: 1790 us
  waiting for transfers between devices  1040 us (57%)
  starting transfers between devices  296 us (16%)
  other arithmetic  145 us (8%)
  local copies, waits for them, and re-layouts  139 us (8%)
  matrix products  118 us (6%)
  Pallas kernels  31.7 us (2%)
  between operations  21.8 us (1%)
    all_to_all x13, waiting for transfers between devices, exchange(): return lax.all_to_all(value, 'row', split_axis=0, concat_axis=0, tiled=True)  1030 us
    all_to_all x13, starting transfers between devices, exchange(): return lax.all_to_all(value, 'row', split_axis=0, concat_axis=0, tiled=True)  296 us
    dot_general x4, matrix products, in_chunks(): jnp.einsum('cd,cwi->dwi', proj_weight[layer_idx], normed_in, preferred_el...  68.8 us
    dot_general x4, matrix products, in_chunks(): jnp.einsum('cd,cwi->dwi', out_weight[layer_idx], normed_out, preferred_el...  40.5 us
  transfers between devices with their start and end apart: 15, of which 15 were waited for; matrix products, arithmetic and copies ran while one was open for 9% of the time, Pallas kernels for 2%

profile of v2, /device:TPU:0, one launch (start us, length us, event | category | flops | bytes accessed | tf_op | source)
XLA Modules:
  0.0 1792.6 jit_solution(15762765570314631739)
XLA Ops:
  31.3 26.0 %copy.45 = bf16[1024,64,128]{2,1,0:T(8,128)(2,1)} copy(bf16[1024,64,128]{0,1,2:T(8,128)(2,1)} %bitcast.24) | data formatting | bytes 33554432 | tf_op jit(solution)/shard_map/transpose | solution.py:104
  87.5 293.6 %all-to-all-done = bf16[16,64,64,128]{3,2,1,0:T(8,128)(2,1)} async-done(((bf16[16,64,64,128]{3,2,1,0:T(8,128)(2,1)}), bf16[16,64,64,128]{3,2,1,0:T(8,128)(2,1)}, u32[]{:S(2)}, u32[]{:S(2)}) %all-to-all-start) | async-done | bytes 16777248 | tf_op jit(solution)/shard_map/all_to_all | solution.py:68
  430.9 73.2 %all-to-all-start.6 = ((bf16[16,4,64,512]{3,2,1,0:T(8,128)(2,1)}), bf16[16,4,64,512]{3,2,1,0:T(8,128)(2,1)}, u32[]{:S(2)}, u32[]{:S(2)}) async-start(bf16[16,4,64,512]{3,2,1,0:T(8,128)(2,1)} %bitcast.178), calls=%async_computation.6 | async-start | bytes 8388608 | tf_op jit(solution)/shard_map/all_to_all | solution.py:68
  510.7 71.9 %all-to-all-done.6.left_ref = bf16[16,4,64,512]{3,2,1,0:T(8,128)(2,1)} async-done(((bf16[16,4,64,512]{3,2,1,0:T(8,128)(2,1)}), bf16[16,4,64,512]{3,2,1,0:T(8,128)(2,1)}, u32[]{:S(2)}, u32[]{:S(2)}) %all-to-all-start.6) | async-done | bytes 4194336 | tf_op jit(solution)/shard_map/all_to_all | solution.py:68
  642.8 37.2 %all-to-all-done.2.refs_0_ = bf16[16,4,64,512]{3,2,1,0:T(8,128)(2,1)} async-done(((bf16[16,4,64,512]{3,2,1,0:T(8,128)(2,1)}), bf16[16,4,64,512]{3,2,1,0:T(8,128)(2,1)}, u32[]{:S(2)}, u32[]{:S(2)}) %all-to-all-start.2) | async-done | bytes 4194336 | tf_op jit(solution)/shard_map/all_to_all | solution.py:68
  680.0 19.5 %all-to-all-start.3 = ((bf16[16,4,64,512]{3,2,1,0:T(8,128)(2,1)}), bf16[16,4,64,512]{3,2,1,0:T(8,128)(2,1)}, u32[]{:S(2)}, u32[]{:S(2)}) async-start(bf16[16,4,64,512]{3,2,1,0:T(8,128)(2,1)} %bitcast.173), calls=%async_computation.3 | async-start | bytes 8388608 | tf_op jit(solution)/shard_map/all_to_all | solution.py:68
  706.0 71.9 %all-to-all-done.3.refs_1_ = bf16[16,4,64,512]{3,2,1,0:T(8,128)(2,1)} async-done(((bf16[16,4,64,512]{3,2,1,0:T(8,128)(2,1)}), bf16[16,4,64,512]{3,2,1,0:T(8,128)(2,1)}, u32[]{:S(2)}, u32[]{:S(2)}) %all-to-all-start.3) | async-done | bytes 4194336 | tf_op jit(solution)/shard_map/all_to_all | solution.py:68
  777.9 19.7 %all-to-all-start.1 = ((bf16[16,4,64,512]{3,2,1,0:T(8,128)(2,1)}), bf16[16,4,64,512]{3,2,1,0:T(8,128)(2,1)}, u32[]{:S(2)}, u32[]{:S(2)}) async-start(bf16[16,4,64,512]{3,2,1,0:T(8,128)(2,1)} %bitcast.176), calls=%async_computation.1 | async-start | bytes 8388608 | tf_op jit(solution)/shard_map/all_to_all | solution.py:68
  807.5 68.5 %all-to-all-done.1.left_ref = bf16[16,4,64,512]{3,2,1,0:T(8,128)(2,1)} async-done(((bf16[16,4,64,512]{3,2,1,0:T(8,128)(2,1)}), bf16[16,4,64,512]{3,2,1,0:T(8,128)(2,1)}, u32[]{:S(2)}, u32[]{:S(2)}) %all-to-all-start.1) | async-done | bytes 4194336 | tf_op jit(solution)/shard_map/all_to_all | solution.py:68
  905.4 68.5 %all-to-all-done.7 = bf16[16,4,64,512]{3,2,1,0:T(8,128)(2,1)} async-done(((bf16[16,4,64,512]{3,2,1,0:T(8,128)(2,1)}), bf16[16,4,64,512]{3,2,1,0:T(8,128)(2,1)}, u32[]{:S(2)}, u32[]{:S(2)}) %all-to-all-start.7) | async-done | bytes 4194336 | tf_op jit(solution)/shard_map/all_to_all | solution.py:68
  973.9 19.5 %all-to-all-start.4 = ((bf16[16,4,64,512]{3,2,1,0:T(8,128)(2,1)}), bf16[16,4,64,512]{3,2,1,0:T(8,128)(2,1)}, u32[]{:S(2)}, u32[]{:S(2)}) async-start(bf16[16,4,64,512]{3,2,1,0:T(8,128)(2,1)} %copy-done.2), calls=%async_computation.4 | async-start | bytes 8388608 | tf_op jit(solution)/shard_map/all_to_all | solution.py:68
  1000.3 71.6 %all-to-all-done.4 = bf16[16,4,64,512]{3,2,1,0:T(8,128)(2,1)} async-done(((bf16[16,4,64,512]{3,2,1,0:T(8,128)(2,1)}), bf16[16,4,64,512]{3,2,1,0:T(8,128)(2,1)}, u32[]{:S(2)}, u32[]{:S(2)}) %all-to-all-start.4) | async-done | bytes 4194336 | tf_op jit(solution)/shard_map/all_to_all | solution.py:68
  1134.3 19.6 %all-to-all-start.9 = ((bf16[16,4,64,512]{3,2,1,0:T(8,128)(2,1)}), bf16[16,4,64,512]{3,2,1,0:T(8,128)(2,1)}, u32[]{:S(2)}, u32[]{:S(2)}) async-start(bf16[16,4,64,512]{3,2,1,0:T(8,128)(2,1)} %bitcast.171), calls=%async_computation.9 | async-start | bytes 8388608 | tf_op jit(solution)/shard_map/all_to_all | solution.py:68
  1209.2 23.2 %all-to-all-done.9.refs_1_ = bf16[16,4,64,512]{3,2,1,0:T(8,128)(2,1)} async-done(((bf16[16,4,64,512]{3,2,1,0:T(8,128)(2,1)}), bf16[16,4,64,512]{3,2,1,0:T(8,128)(2,1)}, u32[]{:S(2)}, u32[]{:S(2)}) %all-to-all-start.9) | async-done | bytes 4194336 | tf_op jit(solution)/shard_map/all_to_all | solution.py:68
  1258.3 72.0 %all-to-all-done.11.left_ref = bf16[16,4,64,512]{3,2,1,0:T(8,128)(2,1)} async-done(((bf16[16,4,64,512]{3,2,1,0:T(8,128)(2,1)}), bf16[16,4,64,512]{3,2,1,0:T(8,128)(2,1)}, u32[]{:S(2)}, u32[]{:S(2)}) %all-to-all-start.11) | async-done | bytes 4194336 | tf_op jit(solution)/shard_map/all_to_all | solution.py:68
  1330.3 19.5 %all-to-all-start.8 = ((bf16[16,4,64,512]{3,2,1,0:T(8,128)(2,1)}), bf16[16,4,64,512]{3,2,1,0:T(8,128)(2,1)}, u32[]{:S(2)}, u32[]{:S(2)}) async-start(bf16[16,4,64,512]{3,2,1,0:T(8,128)(2,1)} %bitcast.175), calls=%async_computation.8 | async-start | bytes 8388608 | tf_op jit(solution)/shard_map/all_to_all | solution.py:68
  1356.4 71.9 %all-to-all-done.8.refs_0_ = bf16[16,4,64,512]{3,2,1,0:T(8,128)(2,1)} async-done(((bf16[16,4,64,512]{3,2,1,0:T(8,128)(2,1)}), bf16[16,4,64,512]{3,2,1,0:T(8,128)(2,1)}, u32[]{:S(2)}, u32[]{:S(2)}) %all-to-all-start.8) | async-done | bytes 4194336 | tf_op jit(solution)/shard_map/all_to_all | solution.py:68
  1428.3 19.5 %all-to-all-start.5 = ((bf16[16,4,64,512]{3,2,1,0:T(8,128)(2,1)}), bf16[16,4,64,512]{3,2,1,0:T(8,128)(2,1)}, u32[]{:S(2)}, u32[]{:S(2)}) async-start(bf16[16,4,64,512]{3,2,1,0:T(8,128)(2,1)} %bitcast.177), calls=%async_computation.5 | async-start | bytes 8388608 | tf_op jit(solution)/shard_map/all_to_all | solution.py:68
  1457.7 68.5 %all-to-all-done.5.left_ref = bf16[16,4,64,512]{3,2,1,0:T(8,128)(2,1)} async-done(((bf16[16,4,64,512]{3,2,1,0:T(8,128)(2,1)}), bf16[16,4,64,512]{3,2,1,0:T(8,128)(2,1)}, u32[]{:S(2)}, u32[]{:S(2)}) %all-to-all-start.5) | async-done | bytes 4194336 | tf_op jit(solution)/shard_map/all_to_all | solution.py:68
  1526.2 19.5 %all-to-all-start.12 = ((bf16[16,4,64,512]{3,2,1,0:T(8,128)(2,1)}), bf16[16,4,64,512]{3,2,1,0:T(8,128)(2,1)}, u32[]{:S(2)}, u32[]{:S(2)}) async-start(bf16[16,4,64,512]{3,2,1,0:T(8,128)(2,1)} %copy-done.4), calls=%async_computation.12 | async-start | bytes 8388608 | tf_op jit(solution)/shard_map/all_to_all | solution.py:68
  1555.6 68.6 %all-to-all-done.12 = bf16[16,4,64,512]{3,2,1,0:T(8,128)(2,1)} async-done(((bf16[16,4,64,512]{3,2,1,0:T(8,128)(2,1)}), bf16[16,4,64,512]{3,2,1,0:T(8,128)(2,1)}, u32[]{:S(2)}, u32[]{:S(2)}) %all-to-all-start.12) | async-done | bytes 4194336 | tf_op jit(solution)/shard_map/all_to_all | solution.py:68
  1624.2 19.5 %all-to-all-start.10 = ((bf16[16,4,64,512]{3,2,1,0:T(8,128)(2,1)}), bf16[16,4,64,512]{3,2,1,0:T(8,128)(2,1)}, u32[]{:S(2)}, u32[]{:S(2)}) async-start(bf16[16,4,64,512]{3,2,1,0:T(8,128)(2,1)} %copy-done.1), calls=%async_computation.10 | async-start | bytes 8388608 | tf_op jit(solution)/shard_map/all_to_all | solution.py:68
  1679.6 42.5 %all-to-all-done.10 = bf16[16,4,64,512]{3,2,1,0:T(8,128)(2,1)} async-done(((bf16[16,4,64,512]{3,2,1,0:T(8,128)(2,1)}), bf16[16,4,64,512]{3,2,1,0:T(8,128)(2,1)}, u32[]{:S(2)}, u32[]{:S(2)}) %all-to-all-start.10) | async-done | bytes 4194336 | tf_op jit(solution)/shard_map/all_to_all | solution.py:68
  1769.1 23.3 %copy.60 = bf16[128,64,1024]{2,1,0:T(8,128)(2,1)} copy(bf16[128,64,1024]{0,2,1:T(8,128)(2,1)} %pad_maximum_fusion) | data formatting | bytes 33554432 | tf_op jit(solution)/shard_map/concatenate | solution.py:148
  (161 shorter events, 462.2 us)
Async XLA Ops:
  0.0 1749.2 %copy-start = (bf16[64,128]{1,0:T(8,128)(2,1)S(1)}, bf16[64,128]{1,0:T(8,128)(2,1)}, u32[]{:S(2)}) copy-start(bf16[64,128]{1,0:T(8,128)(2,1)} %param.11) | copy-start | bytes 49156
  57.4 323.8 %all-to-all-start = ((bf16[16,64,64,128]{3,2,1,0:T(8,128)(2,1)}), bf16[16,64,64,128]{3,2,1,0:T(8,128)(2,1)}, u32[]{:S(2)}, u32[]{:S(2)}) async-start(bf16[16,64,64,128]{3,2,1,0:T(8,128)(2,1)} %bitcast.168), calls=%async_computation | async-start | bytes 33554432 | tf_op jit(solution)/shard_map/all_to_all | solution.py:68
  87.5 323.1 %copy-start.21 = (f32[64,512]{1,0:T(8,128)}, f32[64,512]{1,0:T(8,128)S(1)}, u32[]{:S(2)}) copy-start(f32[64,512]{1,0:T(8,128)S(1)} %get-tuple-element.25) | copy-start | bytes 393220
  386.6 24.0 %copy-start.9 = (bf16[64,64,128]{2,1,0:T(8,128)(2,1)}, bf16[64,64,128]{2,1,0:T(8,128)(2,1)S(1)}, u32[]{:S(2)}) copy-start(bf16[64,64,128]{2,1,0:T(8,128)(2,1)S(1)} %get-tuple-element.19) | copy-start | bytes 3145732
  386.6 24.0 %copy-start.11 = (bf16[64,64,128]{2,1,0:T(8,128)(2,1)}, bf16[64,64,128]{2,1,0:T(8,128)(2,1)S(1)}, u32[]{:S(2)}) copy-start(bf16[64,64,128]{2,1,0:T(8,128)(2,1)S(1)} %get-tuple-element.20) | copy-start | bytes 3145732
  430.9 151.7 %all-to-all-start.6 = ((bf16[16,4,64,512]{3,2,1,0:T(8,128)(2,1)}), bf16[16,4,64,512]{3,2,1,0:T(8,128)(2,1)}, u32[]{:S(2)}, u32[]{:S(2)}) async-start(bf16[16,4,64,512]{3,2,1,0:T(8,128)(2,1)} %bitcast.178), calls=%async_computation.6 | async-start | bytes 8388608 | tf_op jit(solution)/shard_map/all_to_all | solution.py:68
  504.1 97.4 %copy-start.27 = (f32[64,512]{1,0:T(8,128)S(1)}, f32[64,512]{1,0:T(8,128)}, u32[]{:S(2)}) copy-start(f32[64,512]{1,0:T(8,128)} %get-tuple-element.44) | copy-start | bytes 393220
  510.7 94.2 %copy-start.28 = (bf16[2,64,320]{2,1,0:T(8,128)(2,1)S(1)}, bf16[2,64,320]{2,1,0:T(8,128)(2,1)}, u32[]{:S(2)}) copy-start(bf16[2,64,320]{2,1,0:T(8,128)(2,1)} %param.9) | copy-start | bytes 245764
  582.6 97.4 %all-to-all-start.2 = ((bf16[16,4,64,512]{3,2,1,0:T(8,128)(2,1)}), bf16[16,4,64,512]{3,2,1,0:T(8,128)(2,1)}, u32[]{:S(2)}, u32[]{:S(2)}) async-start(bf16[16,4,64,512]{3,2,1,0:T(8,128)(2,1)} %bitcast.172), calls=%async_computation.2 | async-start | bytes 8388608 | tf_op jit(solution)/shard_map/all_to_all | solution.py:68
  680.0 97.9 %all-to-all-start.3 = ((bf16[16,4,64,512]{3,2,1,0:T(8,128)(2,1)}), bf16[16,4,64,512]{3,2,1,0:T(8,128)(2,1)}, u32[]{:S(2)}, u32[]{:S(2)}) async-start(bf16[16,4,64,512]{3,2,1,0:T(8,128)(2,1)} %bitcast.173), calls=%async_computation.3 | async-start | bytes 8388608 | tf_op jit(solution)/shard_map/all_to_all | solution.py:68
  777.9 98.1 %all-to-all-start.1 = ((bf16[16,4,64,512]{3,2,1,0:T(8,128)(2,1)}), bf16[16,4,64,512]{3,2,1,0:T(8,128)(2,1)}, u32[]{:S(2)}, u32[]{:S(2)}) async-start(bf16[16,4,64,512]{3,2,1,0:T(8,128)(2,1)} %bitcast.176), calls=%async_computation.1 | async-start | bytes 8388608 | tf_op jit(solution)/shard_map/all_to_all | solution.py:68
  876.0 97.9 %all-to-all-start.7 = ((bf16[16,4,64,512]{3,2,1,0:T(8,128)(2,1)}), bf16[16,4,64,512]{3,2,1,0:T(8,128)(2,1)}, u32[]{:S(2)}, u32[]{:S(2)}) async-start(bf16[16,4,64,512]{3,2,1,0:T(8,128)(2,1)} %copy-done.3), calls=%async_computation.7 | async-start | bytes 8388608 | tf_op jit(solution)/shard_map/all_to_all | solution.py:68
  973.9 98.0 %all-to-all-start.4 = ((bf16[16,4,64,512]{3,2,1,0:T(8,128)(2,1)}), bf16[16,4,64,512]{3,2,1,0:T(8,128)(2,1)}, u32[]{:S(2)}, u32[]{:S(2)}) async-start(bf16[16,4,64,512]{3,2,1,0:T(8,128)(2,1)} %copy-done.2), calls=%async_computation.4 | async-start | bytes 8388608 | tf_op jit(solution)/shard_map/all_to_all | solution.py:68
  996.3 85.3 %copy-start.24 = (f32[64,512]{1,0:T(8,128)}, f32[64,512]{1,0:T(8,128)S(1)}, u32[]{:S(2)}) copy-start(f32[64,512]{1,0:T(8,128)S(1)} %broadcast_multiply_fusion.6) | copy-start | bytes 393220
  1127.8 26.2 %copy-start.25 = (f32[64,512]{1,0:T(8,128)S(1)}, f32[64,512]{1,0:T(8,128)}, u32[]{:S(2)}) copy-start(f32[64,512]{1,0:T(8,128)} %copy-done.24) | copy-start | bytes 393220
  1127.8 26.2 %copy-start.26 = (f32[64,512]{1,0:T(8,128)S(1)}, f32[64,512]{1,0:T(8,128)}, u32[]{:S(2)}) copy-start(f32[64,512]{1,0:T(8,128)} %add_rsqrt_fusion.5) | copy-start | bytes 393220
  1134.3 98.1 %all-to-all-start.9 = ((bf16[16,4,64,512]{3,2,1,0:T(8,128)(2,1)}), bf16[16,4,64,512]{3,2,1,0:T(8,128)(2,1)}, u32[]{:S(2)}, u32[]{:S(2)}) async-start(bf16[16,4,64,512]{3,2,1,0:T(8,128)(2,1)} %bitcast.171), calls=%async_computation.9 | async-start | bytes 8388608 | tf_op jit(solution)/shard_map/all_to_all | solution.py:68
  1232.4 97.9 %all-to-all-start.11 = ((bf16[16,4,64,512]{3,2,1,0:T(8,128)(2,1)}), bf16[16,4,64,512]{3,2,1,0:T(8,128)(2,1)}, u32[]{:S(2)}, u32[]{:S(2)}) async-start(bf16[16,4,64,512]{3,2,1,0:T(8,128)(2,1)} %bitcast.174), calls=%async_computation.11 | async-start | bytes 8388608 | tf_op jit(solution)/shard_map/all_to_all | solution.py:68
  1330.3 97.9 %all-to-all-start.8 = ((bf16[16,4,64,512]{3,2,1,0:T(8,128)(2,1)}), bf16[16,4,64,512]{3,2,1,0:T(8,128)(2,1)}, u32[]{:S(2)}, u32[]{:S(2)}) async-start(bf16[16,4,64,512]{3,2,1,0:T(8,128)(2,1)} %bitcast.175), calls=%async_computation.8 | async-start | bytes 8388608 | tf_op jit(solution)/shard_map/all_to_all | solution.py:68
  1428.3 97.9 %all-to-all-start.5 = ((bf16[16,4,64,512]{3,2,1,0:T(8,128)(2,1)}), bf16[16,4,64,512]{3,2,1,0:T(8,128)(2,1)}, u32[]{:S(2)}, u32[]{:S(2)}) async-start(bf16[16,4,64,512]{3,2,1,0:T(8,128)(2,1)} %bitcast.177), calls=%async_computation.5 | async-start | bytes 8388608 | tf_op jit(solution)/shard_map/all_to_all | solution.py:68
  1526.2 97.9 %all-to-all-start.12 = ((bf16[16,4,64,512]{3,2,1,0:T(8,128)(2,1)}), bf16[16,4,64,512]{3,2,1,0:T(8,128)(2,1)}, u32[]{:S(2)}, u32[]{:S(2)}) async-start(bf16[16,4,64,512]{3,2,1,0:T(8,128)(2,1)} %copy-done.4), calls=%async_computation.12 | async-start | bytes 8388608 | tf_op jit(solution)/shard_map/all_to_all | solution.py:68
  1624.2 97.9 %all-to-all-start.10 = ((bf16[16,4,64,512]{3,2,1,0:T(8,128)(2,1)}), bf16[16,4,64,512]{3,2,1,0:T(8,128)(2,1)}, u32[]{:S(2)}, u32[]{:S(2)}) async-start(bf16[16,4,64,512]{3,2,1,0:T(8,128)(2,1)} %copy-done.1), calls=%async_computation.10 | async-start | bytes 8388608 | tf_op jit(solution)/shard_map/all_to_all | solution.py:68
  1666.8 7.2 collective-permute-start
  1749.2 7.5 collective-permute-start.1
  (25 other events, 277.0 us)
